TPU v7x, 32 devices: a whole 2x2x4 slice. The times are simulated.
32 devices in a mesh: dp: 8 (over y, x, core), seq: 4 (over z).
Axes of the slice: x: 2, y: 2, z: 4, core: 2. Of those that a mesh axis runs over, the one named last changes fastest.
Arguments:
- layer_input: bfloat16 [16, 512, 768], P('dp', 'seq'), may hold values from -6 to 6
- segment_ids: int32 [16, 512], P('dp', 'seq'), may hold values from 0 to 2, as said below
- w_query: bfloat16 [768, 768], replicated, may hold values from -0.21875 to 0.21875
- b_query: float32 [768], replicated, may hold values from -1.5 to 1.5
- w_key: bfloat16 [768, 768], replicated, may hold values from -0.21875 to 0.21875
- w_value: bfloat16 [768, 768], replicated, may hold values from -0.21875 to 0.21875
- b_value: float32 [768], replicated, may hold values from -1.5 to 1.5
- w_out: bfloat16 [768, 768], replicated, may hold values from -1.75 to 1.75
- b_out: float32 [768], replicated, may hold values from -1.5 to 1.5
- gain_one: float32 [768], replicated, may hold values from 0.5 to 1.5
- shift_one: float32 [768], replicated, may hold values from -1.5 to 1.5
- w_inner: bfloat16 [768, 3072], replicated, may hold values from -0.21875 to 0.21875
- b_inner: float32 [3072], replicated, may hold values from -1.5 to 1.5
- w_outer: bfloat16 [3072, 768], replicated, may hold values from -0.109375 to 0.109375
- b_outer: float32 [768], replicated, may hold values from -1.5 to 1.5
- gain_two: float32 [768], replicated, may hold values from 0.5 to 1.5
- shift_two: float32 [768], replicated, may hold values from -1.5 to 1.5
- cotangent: bfloat16 [16, 512, 768], P('dp', 'seq'), may hold values from -6 to 6
Outputs:
- output: bfloat16 [16, 512, 768], P('dp', 'seq')
- d_input: bfloat16 [16, 512, 768], P('dp', 'seq')
- d_w_query: float32 [768, 768], replicated
- d_b_query: float32 [768], replicated
- d_w_key: float32 [768, 768], replicated
- d_w_value: float32 [768, 768], replicated
- d_b_value: float32 [768], replicated
- d_w_out: float32 [768, 768], replicated
- d_b_out: float32 [768], replicated
- d_gain_one: float32 [768], replicated
- d_shift_one: float32 [768], replicated
- d_w_inner: float32 [768, 3072], replicated
- d_b_inner: float32 [3072], replicated
- d_w_outer: float32 [3072, 768], replicated
- d_b_outer: float32 [768], replicated
- d_gain_two: float32 [768], replicated
- d_shift_two: float32 [768], replicated
Inputs may be any that keep to these rules, and one draw needn't show every extreme that they name: `segment_ids`: each row holds either one pair (ids 1, then 0 for padding at its end) of more than 256 tokens, or two pairs packed in halves of 256 positions (ids 1 in the first half, 2 in the second, each followed by padding 0 in its half), each of 128 tokens or more. Some row is a single pair without padding, some row is packed with padding.
All inputs are finite; a program needn't handle non-finite values.
Results may differ from a plain program's by a relative error of at most 0.015.
Values may be sent and summed in bfloat16 or wider, within the bound.
A program may use at most 192 MiB of HBM per device.

v0:
```python
import math
import jax
import jax.numpy as jnp
from jax import lax
from jax.sharding import PartitionSpec as P

HD = 64
EPSILON = 1e-12
MASKED = -1000000000.0
INV_ROOT_TWO = 0.7071067811865476
DENSITY = 0.3989422804014327


def product(left, right):
    return jnp.dot(left, right, preferred_element_type=jnp.float32)


def product_tn(left, right):
    return lax.dot_general(
        left, right, (((0,), (0,)), ((), ())), preferred_element_type=jnp.float32
    )


def product_nt(left, right):
    return lax.dot_general(
        left, right, (((1,), (1,)), ((), ())), preferred_element_type=jnp.float32
    )


def layer_norm(values, scale_gain, offset):
    centre = values - jnp.mean(values, axis=-1, keepdims=True)
    inverse_std = lax.rsqrt(jnp.mean(centre * centre, axis=-1, keepdims=True) + EPSILON)
    normed = centre * inverse_std
    return (normed * scale_gain + offset, normed, inverse_std)


def norm_back(grad_out, normed, inverse_std, scale_gain):
    scaled = grad_out * scale_gain
    return inverse_std * (
        scaled
        - jnp.mean(scaled, axis=-1, keepdims=True)
        - normed * jnp.mean(scaled * normed, axis=-1, keepdims=True)
    )


def split_heads(tensor):
    return tensor.reshape(tensor.shape[0], tensor.shape[1], tensor.shape[2] // HD, HD)


def grouped(tensor, group):
    return tensor.reshape((tensor.shape[0] // group, group) + tensor.shape[1:])


def ungrouped(tensor):
    return tensor.reshape((tensor.shape[0] * tensor.shape[1],) + tensor.shape[2:])


def masked_scores(query_rows, key_rows, query_segs, key_segs):
    scores = (
        jnp.einsum(
            "rqhd,rkhd->rhqk",
            split_heads(query_rows),
            split_heads(key_rows),
            preferred_element_type=jnp.float32,
        )
        * 0.125
    )
    same_pair = query_segs[:, None, :, None] == key_segs[:, None, None, :]
    return jnp.where(same_pair, scores, MASKED)


def attend(packed_item):
    query_rows, key_rows, value_rows, query_segs, key_segs = packed_item
    scores = masked_scores(query_rows, key_rows, query_segs, key_segs)
    row_max = jnp.max(scores, axis=-1, keepdims=True)
    powers = jnp.exp(scores - row_max)
    totals = jnp.sum(powers, axis=-1, keepdims=True)
    soft_probs = (powers / totals).astype(jnp.bfloat16)
    attended = jnp.einsum(
        "rhqk,rkhd->rqhd", soft_probs, split_heads(value_rows), preferred_element_type=jnp.float32
    )
    return (attended.reshape(query_rows.shape), (row_max + jnp.log(totals))[..., 0])


def attend_back(packed_item):
    query_rows, key_rows, value_rows, query_segs, key_segs, log_total, grad_attn, attended = (
        packed_item
    )
    scores = masked_scores(query_rows, key_rows, query_segs, key_segs)
    probs = jnp.exp(scores - log_total[..., None])
    grad_heads = split_heads(grad_attn)
    delta = jnp.sum(grad_heads.astype(jnp.float32) * split_heads(attended), axis=-1)
    delta = jnp.swapaxes(delta, 1, 2)[..., None]
    grad_prob = jnp.einsum(
        "rqhd,rkhd->rhqk", grad_heads, split_heads(value_rows), preferred_element_type=jnp.float32
    )
    grad_scores = (probs * (grad_prob - delta)).astype(jnp.bfloat16)
    grad_query = (
        jnp.einsum(
            "rhqk,rkhd->rqhd",
            grad_scores,
            split_heads(key_rows),
            preferred_element_type=jnp.float32,
        )
        * 0.125
    )
    grad_keys = (
        jnp.einsum(
            "rhqk,rqhd->rkhd",
            grad_scores,
            split_heads(query_rows),
            preferred_element_type=jnp.float32,
        )
        * 0.125
    )
    grad_values = jnp.einsum(
        "rhqk,rqhd->rkhd",
        probs.astype(jnp.bfloat16),
        grad_heads,
        preferred_element_type=jnp.float32,
    )
    return (
        grad_query.reshape(query_rows.shape),
        grad_keys.reshape(key_rows.shape),
        grad_values.reshape(key_rows.shape),
    )


def on_device(
    layer_input,
    segment_ids,
    w_query,
    b_query,
    w_key,
    w_value,
    b_value,
    w_out,
    b_out,
    gain_one,
    shift_one,
    w_inner,
    b_inner,
    w_outer,
    b_outer,
    gain_two,
    shift_two,
    cotangent,
):
    row_count, shard_len, model_dim = layer_input.shape
    tok_count = row_count * shard_len
    tokens = layer_input.reshape(tok_count, model_dim)
    query_flat = (product(tokens, w_query) + b_query).astype(jnp.bfloat16)
    key_flat = product(tokens, w_key).astype(jnp.bfloat16)
    value_flat = (product(tokens, w_value) + b_value).astype(jnp.bfloat16)
    stacked = jnp.stack([key_flat, value_flat]).reshape(2, row_count, shard_len, model_dim)
    context, seg_context = (
        lax.all_gather(stacked, "seq", axis=2, tiled=True),
        lax.all_gather(segment_ids, "seq", axis=1, tiled=True),
    )
    group = math.gcd(row_count, max(1, 512 // shard_len))
    query_grid = grouped(query_flat.reshape(row_count, shard_len, model_dim), group)
    query_segs = grouped(segment_ids, group)
    key_segs = grouped(seg_context, group)
    attn_grid, log_total = lax.map(
        attend,
        (query_grid, grouped(context[0], group), grouped(context[1], group), query_segs, key_segs),
    )
    attn_low = ungrouped(attn_grid).reshape(tok_count, model_dim).astype(jnp.bfloat16)
    branch = product(attn_low, w_out) + b_out
    hidden_one, normed_one, inverse_one = layer_norm(
        tokens.astype(jnp.float32) + branch, gain_one, shift_one
    )
    hidden_low = hidden_one.astype(jnp.bfloat16)
    inner_pre = product(hidden_low, w_inner) + b_inner
    cdf_part = 0.5 * (1.0 + lax.erf(inner_pre * INV_ROOT_TWO))
    active_low = (inner_pre * cdf_part).astype(jnp.bfloat16)
    outer_out = product(active_low, w_outer) + b_outer
    result, normed_two, inverse_two = layer_norm(hidden_one + outer_out, gain_two, shift_two)
    grad_out = cotangent.reshape(tok_count, model_dim).astype(jnp.float32)
    grad_gain_two = jnp.sum(grad_out * normed_two, axis=0)
    grad_shift_two = jnp.sum(grad_out, axis=0)
    grad_two = norm_back(grad_out, normed_two, inverse_two, gain_two)
    grad_outer = grad_two.astype(jnp.bfloat16)
    grad_w_outer = product_tn(active_low, grad_outer)
    grad_b_outer = jnp.sum(grad_outer.astype(jnp.float32), axis=0)
    grad_active = product_nt(grad_outer, w_outer)
    slope = cdf_part + inner_pre * DENSITY * jnp.exp(-0.5 * inner_pre * inner_pre)
    grad_inner = (grad_active * slope).astype(jnp.bfloat16)
    grad_w_inner = product_tn(hidden_low, grad_inner)
    grad_b_inner = jnp.sum(grad_inner.astype(jnp.float32), axis=0)
    grad_hidden = grad_two + product_nt(grad_inner, w_inner)
    grad_gain_one = jnp.sum(grad_hidden * normed_one, axis=0)
    grad_shift_one = jnp.sum(grad_hidden, axis=0)
    grad_one = norm_back(grad_hidden, normed_one, inverse_one, gain_one)
    grad_branch = grad_one.astype(jnp.bfloat16)
    grad_w_out = product_tn(attn_low, grad_branch)
    grad_b_out = jnp.sum(grad_branch.astype(jnp.float32), axis=0)
    grad_attn = product_nt(grad_branch, w_out).astype(jnp.bfloat16)
    grad_attn_grid = grouped(grad_attn.reshape(row_count, shard_len, model_dim), group)
    query_part, key_part, value_part = lax.map(
        attend_back,
        (
            query_grid,
            grouped(context[0], group),
            grouped(context[1], group),
            query_segs,
            key_segs,
            log_total,
            grad_attn_grid,
            attn_grid,
        ),
    )
    key_home, value_home = (
        lax.psum_scatter(
            ungrouped(key_part).astype(jnp.bfloat16), "seq", scatter_dimension=1, tiled=True
        ).astype(jnp.float32),
        lax.psum_scatter(
            ungrouped(value_part).astype(jnp.bfloat16), "seq", scatter_dimension=1, tiled=True
        ).astype(jnp.float32),
    )
    grad_query = ungrouped(query_part).reshape(tok_count, model_dim).astype(jnp.bfloat16)
    grad_key = key_home.reshape(tok_count, model_dim).astype(jnp.bfloat16)
    grad_value = value_home.reshape(tok_count, model_dim).astype(jnp.bfloat16)
    grad_w_query = product_tn(tokens, grad_query)
    grad_b_query = jnp.sum(grad_query.astype(jnp.float32), axis=0)
    grad_w_key = product_tn(tokens, grad_key)
    grad_w_value = product_tn(tokens, grad_value)
    grad_b_value = jnp.sum(grad_value.astype(jnp.float32), axis=0)
    grad_input = (
        grad_one
        + product_nt(grad_query, w_query)
        + product_nt(grad_key, w_key)
        + product_nt(grad_value, w_value)
    )
    summed = lax.psum(
        (
            grad_w_query,
            grad_b_query,
            grad_w_key,
            grad_w_value,
            grad_b_value,
            grad_w_out,
            grad_b_out,
            grad_w_outer,
            grad_b_outer,
            grad_gain_two,
            grad_shift_two,
            grad_w_inner,
            grad_b_inner,
            grad_gain_one,
            grad_shift_one,
        ),
        ("dp", "seq"),
    )
    return (
        result.reshape(row_count, shard_len, model_dim).astype(jnp.bfloat16),
        grad_input.reshape(row_count, shard_len, model_dim).astype(jnp.bfloat16),
        summed[0],
        summed[1],
        summed[2],
        summed[3],
        summed[4],
        summed[5],
        summed[6],
        summed[13],
        summed[14],
        summed[11],
        summed[12],
        summed[7],
        summed[8],
        summed[9],
        summed[10],
    )


def solution(mesh):
    return jax.shard_map(
        on_device,
        mesh=mesh,
        in_specs=(
            P("dp", "seq", None),
            P("dp", "seq"),
            P(),
            P(),
            P(),
            P(),
            P(),
            P(),
            P(),
            P(),
            P(),
            P(),
            P(),
            P(),
            P(),
            P(),
            P(),
            P("dp", "seq", None),
        ),
        out_specs=(
            P("dp", "seq", None),
            P("dp", "seq", None),
            P(),
            P(),
            P(),
            P(),
            P(),
            P(),
            P(),
            P(),
            P(),
            P(),
            P(),
            P(),
            P(),
            P(),
            P(),
        ),
        check_vma=False,
    )
```

profile of v0, /device:TPU:0, one launch (start us, length us, event | category | flops | bytes accessed | tf_op | source)
XLA Modules:
  0.0 666.1 jit_solution(12733375049098746954)
XLA Ops:
  7.3 2.0 convolution_convert_fusion.1
  9.3 1.8 fusion.20
  11.1 0.9 pad_maximum_fusion
  12.1 0.0 reduce-scatter.3.cloned.1.call-start
  12.2 1.8 fusion.21
  13.9 0.2 copy.43
  14.1 0.1 reshape.206
  14.2 12.6 %all_gather.7 = s32[2,512]{1,0:T(2,128)S(1)} all-gather(s32[2,128]{1,0:T(2,128)S(1)} %copy-done.40), channel_id=1, replica_groups=mesh['dp'=8,'seq'=4] {'seq'}, dimensions={1}, use_global_device_ids=true | all-gather | bytes 5120 | tf_op jit(solution)/shard_map/all_gather | solution.py:158
  26.8 0.7 convert_reduce_fusion.1
  27.6 0.8 broadcast_compare_fusion
  28.3 50.1 %all-gather.2.cloned.1.call-done = bf16[2,2,512,768]{3,2,1,0:T(8,128)(2,1)} async-done(((bf16[2,2,128,768]{3,2,1,0:T(8,128)(2,1)}), bf16[2,2,512,768]{3,2,1,0:T(8,128)(2,1)}) %all-gather.2.cloned.1.call-update) | async-done | bytes 3145744 | tf_op jit(solution)/shard_map/all_gather | solution.py:157
  78.4 3.7 fusion.60
  82.2 1.7 copy.44
  83.9 2.6 copy.42
  86.5 2.3 fusion.3
  88.8 1.8 fusion
  90.6 0.9 log_add_fusion
  91.5 3.1 fusion.61
  94.6 0.4 copy.46
  95.1 0.6 fusion.62
  95.7 0.2 multiply_reduce_fusion.4
  96.0 1.8 multiply_convert_fusion.2
  97.9 1.5 fusion.63
  99.5 0.2 multiply_reduce_fusion.3
  99.7 0.9 fusion.31
  100.7 1.7 convert_reduce_fusion.2
  102.4 3.0 convert_reduce_fusion
  105.4 2.2 multiply_reduce_fusion
  107.6 0.9 convert_reduce_fusion.3
  108.5 1.3 convolution_convert_fusion
  109.8 1.2 copy.47
  110.9 0.1 reshape.208
  111.0 1.2 multiply_reduce_fusion.1
  112.3 4.6 multiply_convert_fusion
  116.9 1.7 copy-done.3
  118.5 1.7 multiply_convert_fusion.1
  120.3 2.6 copy.52
  122.9 0.0 reduce-scatter.5.cloned.1.call-start
  123.0 5.5 fusion.14
  128.5 2.6 copy.54
  131.1 0.0 all-reduce.4.cloned.1.call-start
  131.2 3.2 convert_reduce_fusion.5
  134.4 0.4 copy.50
  134.8 1.9 convolution_bitcast_fusion.2
  136.7 1.9 fusion.35
  138.6 5.2 fusion.49
  143.8 5.3 fusion.56
  149.2 7.9 %reduce-scatter.3.cloned.1.call-done = bf16[2,128,768]{2,1,0:T(8,128)(2,1)} async-done(((bf16[2,512,768]{2,1,0:T(8,128)(2,1)}), bf16[2,128,768]{2,1,0:T(8,128)(2,1)}) %reduce-scatter.3.cloned.1.call-update) | async-done | bytes 393232 | tf_op jit(solution)/shard_map/reduce_scatter | solution.py:214
  157.0 2.9 convolution_bitcast_fusion.1
  160.0 34.3 %reduce-scatter.5.cloned.1.call-done = bf16[2,128,768]{2,1,0:T(8,128)(2,1)} async-done(((bf16[2,512,768]{2,1,0:T(8,128)(2,1)}), bf16[2,128,768]{2,1,0:T(8,128)(2,1)}) %reduce-scatter.5.cloned.1.call-update) | async-done | bytes 393232 | tf_op jit(solution)/shard_map/reduce_scatter | solution.py:217
  194.2 2.9 convolution_bitcast_fusion
  197.2 0.7 reduce_sum.186
  197.9 1.8 convolution_add_fusion.3
  199.7 0.1 convert_reduce_fusion.4
  199.8 42.9 %all-reduce = (f32[768]{0:T(1024)}, f32[768]{0:T(1024)}, f32[768]{0:T(1024)}, f32[768]{0:T(1024)}, f32[768]{0:T(1024)}, /*index=5*/f32[3072]{0:T(1024)}, f32[768]{0:T(1024)}, f32[768]{0:T(1024)}, f32[768]{0:T(1024)}) all-reduce(f32[768]{0:T(1024)S(1)} %copy-done.36, ...), channel_id=1, replica_groups=mesh['dp'=8,'seq'=4] {'dp','seq'}, use_global_device_ids=true, to_apply=%region_15.16 | all-reduce | flops 9216 | bytes 73728 | tf_op jit(solution)/shard_map/psum | solution.py:235
  242.7 1.6 convolution_add_fusion.2
  244.3 1.3 fusion.22
  245.6 391.2 %all-reduce.4.cloned.1.call-done = (f32[768,768]{0,1:T(8,128)}, f32[768,768]{0,1:T(8,128)}, f32[768,768]{0,1:T(8,128)}, f32[768,768]{1,0:T(8,128)}, f32[768,3072]{1,0:T(8,128)}, /*index=5*/f32[3072,768]{1,0:T(8,128)}) async-done(((f32[768,768]{0,1:T(8,128)}, f32[768,768]{0,1:T(8,128)}, f32[768,768]{0,1:T(8,128)}, f32[768,768]{1,0:T(8,128)}, f32[768,3072]{1,0:T(8,128)}, /*index=5*/f32[3072,768]{1,0:T(8,128)}), ...) | async-done | bytes 28311568 | tf_op jit(solution)/shard_map/psum | solution.py:235
  636.7 3.2 copy.57
  639.9 1.9 copy.58
  641.9 3.2 copy.59
  645.1 1.4 copy.99
  646.5 9.3 %copy.100 = f32[768,3072]{1,0:T(8,128)} copy(f32[768,3072]{1,0:T(8,128)} %get-tuple-element.169) | data formatting | bytes 18874368
  655.8 3.7 copy.101
  (118 shorter events, 0.4 us)
Async XLA Ops:
  7.2 87.9 %copy-start = (bf16[768,768]{1,0:T(8,128)(2,1)S(1)}, bf16[768,768]{1,0:T(8,128)(2,1)}, u32[]{:S(2)}) copy-start(bf16[768,768]{1,0:T(8,128)(2,1)} %param.25) | copy-start | bytes 3538948
  7.2 71.2 %all-gather.2.cloned.1.call-start = ((), (), s32[]{:S(2)}) async-start(), calls=%async_computation.2 | async-start | bytes 3932160 | tf_op jit(solution)/shard_map/all_gather | solution.py:157
  7.3 4.9 copy-start.6
  7.3 4.9 copy-start.42
  11.1 3.1 copy-start.40
  11.1 15.7 %copy-start.11 = (bf16[2,128,768]{2,1,0:T(8,128)(2,1)S(1)}, bf16[2,128,768]{2,1,0:T(8,128)(2,1)}, u32[]{:S(2)}) copy-start(bf16[2,128,768]{2,1,0:T(8,128)(2,1)} %param.35) | copy-start | bytes 1179652
  11.1 15.7 %copy-start.30 = (f32[768]{0:T(1024)S(1)}, f32[768]{0:T(1024)}, u32[]{:S(2)}) copy-start(f32[768]{0:T(1024)} %param.33) | copy-start | bytes 9220
  12.1 144.9 %reduce-scatter.3.cloned.1.call-start = ((), (), s32[]{:S(2)}) async-start(), calls=%async_computation.3 | async-start | bytes 1966080 | tf_op jit(solution)/shard_map/reduce_scatter | solution.py:214
  14.2 72.3 %copy-start.9 = (bf16[2,128,12,64]{1,0,3,2:T(2,128)(2,1)}, bf16[2,128,12,64]{1,0,3,2:T(2,128)(2,1)S(1)}, u32[]{:S(2)}) copy-start(bf16[2,128,12,64]{1,0,3,2:T(2,128)(2,1)S(1)} %reshape.206) | copy-start | bytes 1179652
  86.5 2.3 copy-start.25
  88.8 2.7 copy-start.2
  88.8 2.7 copy-start.20
  91.4 4.5 slice-start.5
  91.5 3.6 copy-start.43
  91.5 4.5 slice-start.6
  94.6 1.4 copy-start.28
  94.6 1.4 copy-start.29
  94.6 1.4 copy-start.41
  95.0 0.9 copy-start.21
  95.1 2.8 slice-start.3
  95.7 11.9 %copy-start.4 = (f32[256,768]{1,0:T(8,128)}, f32[256,768]{1,0:T(8,128)S(1)}, u32[]{:S(2)}) copy-start(f32[256,768]{1,0:T(8,128)S(1)} %get-tuple-element.146) | copy-start | bytes 2359300
  95.7 11.9 %copy-start.31 = (f32[256]{0:T(256)}, f32[256]{0:T(256)S(1)}, u32[]{:S(2)}) copy-start(f32[256]{0:T(256)S(1)} %broadcast_multiply_fusion.4) | copy-start | bytes 3076
  96.0 11.6 %copy-start.37 = (f32[256]{0:T(256)}, f32[256]{0:T(256)S(1)}, u32[]{:S(2)}) copy-start(f32[256]{0:T(256)S(1)} %add_rsqrt_fusion.1) | copy-start | bytes 3076
  96.0 1.9 slice-start.4
  96.0 1.9 copy-start.44
  97.9 1.6 copy-start.16
  97.9 1.8 copy-start.12
  97.9 2.8 copy-start.39
  102.4 3.0 copy-start.14
  105.4 2.2 copy-start.23
  112.3 6.3 copy-start.10
  116.9 1.7 copy-start.3
  120.3 2.7 copy-start.26
  120.3 2.7 copy-start.35
  122.9 71.3 %reduce-scatter.5.cloned.1.call-start = ((), (), s32[]{:S(2)}) async-start(), calls=%async_computation.4 | async-start | bytes 1966080 | tf_op jit(solution)/shard_map/reduce_scatter | solution.py:217
  131.1 3.7 copy-start.7
  131.1 505.6 %all-reduce.4.cloned.1.call-start = ((), (), s32[]{:S(2)}) async-start(), calls=%async_computation.5 | async-start | bytes 56623104 | tf_op jit(solution)/shard_map/psum | solution.py:235
  134.4 2.3 copy-start.22
  134.8 3.8 copy-start.15
  134.8 3.8 copy-start.17
  138.6 5.2 copy-start.5
  138.6 5.2 copy-start.24
  138.6 5.2 copy-start.32
  138.6 5.2 copy-start.38
  197.1 2.5 copy-start.13
  197.2 2.6 copy-start.33
  197.2 2.6 copy-start.34
  197.2 45.5 %copy-start.8 = (bf16[768,768]{1,0:T(8,128)(2,1)S(1)}, bf16[768,768]{1,0:T(8,128)(2,1)}, u32[]{:S(2)}) copy-start(bf16[768,768]{1,0:T(8,128)(2,1)} %param.22) | copy-start | bytes 3538948
  197.9 1.9 copy-start.36
  242.7 1.6 copy-start.27
  636.7 3.2 copy-start.19
  641.9 3.2 copy-start.18
  645.1 10.7 %slice-start = ((s8[9437184]{0:T(1024)(128)(4,1)}), s8[4194304]{0:T(1024)(128)(4,1)S(1)}, s32[]{:S(2)}) async-start(s8[9437184]{0:T(1024)(128)(4,1)} %bitcast.106), calls=%async_computation.6 | async-start | bytes 8388608
  646.5 9.3 %slice-start.1 = ((s8[9437184]{0:T(1024)(128)(4,1)}), s8[4194304]{0:T(1024)(128)(4,1)S(1)}, s32[]{:S(2)}) async-start(s8[9437184]{0:T(1024)(128)(4,1)} %bitcast.106), calls=%async_computation.7 | async-start | bytes 8388608
  646.5 9.3 %slice-start.2 = ((s8[9437184]{0:T(1024)(128)(4,1)}), s8[1048576]{0:T(1024)(128)(4,1)S(1)}, s32[]{:S(2)}) async-start(s8[9437184]{0:T(1024)(128)(4,1)} %bitcast.106), calls=%async_computation.8 | async-start | bytes 2097152
  655.8 3.8 copy-start.1
Sparse Core Ops, SparseCore 0:
  12.2 66.1 all-gather.1
  123.0 33.9 reduce-scatter.2
  159.9 34.2 reduce-scatter.4
  201.6 435.0 all-reduce.3
where the time goes:
time: 667 us; the launch traced here: 666 us
  waiting for transfers between devices  483 us (72%)
  matrix products  61.2 us (9%)
  blocking collectives  55.5 us (8%)
  local copies, waits for them, and re-layouts  41 us (6%)
  between operations  14.4 us (2%)
  other arithmetic  10.4 us (2%)
    psum x1, waiting for transfers between devices, on_device(): lax.psum((grad_w_query, grad_b_query, grad_w_key, grad_w_value, grad_b_va...  391 us
    all_gather x1, waiting for transfers between devices, on_device(): lax.all_gather(stacked, 'seq', axis=2, tiled=True)  50.1 us
    psum x1, blocking collectives, on_device(): lax.psum((grad_w_query, grad_b_query, grad_w_key, grad_w_value, grad_b_va...  42.9 us
    reduce_scatter x1, waiting for transfers between devices, on_device(): lax.psum_scatter(ungrouped(value_part).astype(jnp.bfloat16), 'seq', scatt...  34.3 us
    unnamed x110, local copies, waits for them, and re-layouts  24.8 us
    dot_general x6, matrix products, product_tn(): lax.dot_general(left, right, (((0,), (0,)), ((), ())), preferred_element_...  20.1 us
  transfers between devices with their start and end apart: 4, of which 4 were waited for; matrix products, arithmetic and copies ran while one was open for 6% of the time, Pallas kernels for 0%

commit v1 on v0

--- a/solution.py
+++ b/solution.py
@@ -233,24 +233,27 @@
         + product_nt(grad_value, w_value)
     )
     summed = lax.psum(
-        (
-            grad_w_query,
-            grad_b_query,
-            grad_w_key,
-            grad_w_value,
-            grad_b_value,
-            grad_w_out,
-            grad_b_out,
-            grad_w_outer,
-            grad_b_outer,
-            grad_gain_two,
-            grad_shift_two,
-            grad_w_inner,
-            grad_b_inner,
-            grad_gain_one,
-            grad_shift_one,
+        lax.psum(
+            (
+                grad_w_query,
+                grad_b_query,
+                grad_w_key,
+                grad_w_value,
+                grad_b_value,
+                grad_w_out,
+                grad_b_out,
+                grad_w_outer,
+                grad_b_outer,
+                grad_gain_two,
+                grad_shift_two,
+                grad_w_inner,
+                grad_b_inner,
+                grad_gain_one,
+                grad_shift_one,
+            ),
+            "seq",
         ),
-        ("dp", "seq"),
+        "dp",
     )
     return (
         result.reshape(row_count, shard_len, model_dim).astype(jnp.bfloat16),

time: 667 us -> 1520 us (2.28)
  waiting for transfers between devices: 483 us -> 1340 us
    psum x1, waiting for transfers between devices: 391 us -> 941 us  [on_device(): lax.psum((grad_w_query, grad_b_query, grad_w_key, grad_w_value, grad_b_va...]
    psum x0 -> x1, waiting for transfers between devices: none -> 301 us  [on_device(): lax.psum(lax.psum((grad_w_query, grad_b_query, grad_w_key, grad_w_value,...]
    psum x0 -> x1, blocking collectives: none -> 25.9 us  [on_device(): lax.psum(lax.psum((grad_w_query, grad_b_query, grad_w_key, grad_w_value,...]
    psum x1, blocking collectives: 42.9 us -> 18.1 us  [on_device(): lax.psum((grad_w_query, grad_b_query, grad_w_key, grad_w_value, grad_b_va...]
  transfers between devices with their start and end apart: 4 -> 5, of which waited for: 4 -> 5; matrix products, arithmetic and copies ran while one was open for 6% -> 2% of each run, Pallas kernels for 0% -> 0%
where the time goes in v1:
time: 1520 us
  waiting for transfers between devices  1340 us (88%)
  matrix products  59.9 us (4%)
  blocking collectives  56.5 us (4%)
  local copies, waits for them, and re-layouts  41 us (3%)
    psum x1, waiting for transfers between devices, on_device(): lax.psum((grad_w_query, grad_b_query, grad_w_key, grad_w_value, grad_b_va...  941 us
    psum x1, waiting for transfers between devices, on_device(): lax.psum(lax.psum((grad_w_query, grad_b_query, grad_w_key, grad_w_value,...  301 us
    all_gather x1, waiting for transfers between devices, on_device(): lax.all_gather(stacked, 'seq', axis=2, tiled=True)  51.3 us
    reduce_scatter x1, waiting for transfers between devices, on_device(): lax.psum_scatter(ungrouped(value_part).astype(jnp.bfloat16), 'seq', scatt...  34.3 us
  transfers between devices with their start and end apart: 5, of which 5 were waited for; matrix products, arithmetic and copies ran while one was open for 2% of the time, Pallas kernels for 0%

profile of v1, /device:TPU:0, one launch (start us, length us, event | category | flops | bytes accessed | tf_op | source)
XLA Modules:
  0.0 1518.0 jit_solution(1093609214717297814)
XLA Ops:
  7.3 2.0 convolution_convert_fusion.1
  9.3 1.8 fusion.20
  11.2 0.9 pad_maximum_fusion
  12.2 0.5 fusion.21
  12.7 0.2 copy.43
  12.9 0.1 reshape.206
  13.0 12.6 all_gather.7
  25.6 0.7 convert_reduce_fusion.1
  26.3 0.8 broadcast_compare_fusion
  27.1 51.3 %all-gather.2.cloned.1.call-done = bf16[2,2,512,768]{3,2,1,0:T(8,128)(2,1)} async-done(((bf16[2,2,128,768]{3,2,1,0:T(8,128)(2,1)}), bf16[2,2,512,768]{3,2,1,0:T(8,128)(2,1)}) %all-gather.2.cloned.1.call-update) | async-done | bytes 3145744 | tf_op jit(solution)/shard_map/all_gather | solution.py:157
  78.5 3.7 fusion.60
  82.2 1.7 copy.44
  83.9 2.6 copy.42
  86.5 2.3 fusion.3
  88.9 1.8 fusion
  90.6 0.9 log_add_fusion
  91.5 3.1 fusion.61
  94.7 0.4 copy.46
  95.1 0.6 fusion.62
  95.7 0.2 multiply_reduce_fusion.4
  96.1 1.8 multiply_convert_fusion.2
  98.0 1.5 fusion.63
  99.6 0.2 multiply_reduce_fusion.3
  99.8 0.9 fusion.31
  100.7 1.7 convert_reduce_fusion.2
  102.4 3.0 convert_reduce_fusion
  105.4 2.2 multiply_reduce_fusion
  107.7 0.9 convert_reduce_fusion.3
  108.5 1.3 convolution_convert_fusion
  109.8 1.2 copy.47
  111.0 0.1 reshape.208
  111.1 1.2 multiply_reduce_fusion.1
  112.3 4.6 multiply_convert_fusion
  117.0 1.7 copy-done.3
  118.6 1.7 multiply_convert_fusion.1
  120.3 2.6 copy.52
  123.0 5.5 fusion.14
  128.6 2.6 copy.54
  131.2 0.0 all-reduce.9.cloned.1.call-start
  131.2 3.2 convert_reduce_fusion.5
  134.4 0.4 copy.50
  134.9 1.9 convolution_bitcast_fusion.2
  136.8 1.9 fusion.35
  138.7 5.2 fusion.49
  143.9 5.3 fusion.56
  149.2 7.9 reduce-scatter.3.cloned.1.call-done
  157.1 2.9 convolution_bitcast_fusion.1
  160.0 34.3 %reduce-scatter.5.cloned.1.call-done = bf16[2,128,768]{2,1,0:T(8,128)(2,1)} async-done(((bf16[2,512,768]{2,1,0:T(8,128)(2,1)}), bf16[2,128,768]{2,1,0:T(8,128)(2,1)}) %reduce-scatter.5.cloned.1.call-update) | async-done | bytes 393232 | tf_op jit(solution)/shard_map/reduce_scatter | solution.py:217
  194.3 2.9 convolution_bitcast_fusion
  197.3 940.9 %all-reduce.9.cloned.1.call-done = (f32[768,768]{0,1:T(8,128)}, f32[768,768]{0,1:T(8,128)}, f32[768,768]{0,1:T(8,128)}, f32[768,768]{1,0:T(8,128)}, f32[768,3072]{1,0:T(8,128)}, /*index=5*/f32[3072,768]{1,0:T(8,128)}) async-done(((f32[768,768]{0,1:T(8,128)}, f32[768,768]{0,1:T(8,128)}, f32[768,768]{0,1:T(8,128)}, f32[768,768]{1,0:T(8,128)}, f32[768,3072]{1,0:T(8,128)}, /*index=5*/f32[3072,768]{1,0:T(8,128)}), ...) | async-done | bytes 28311568 | tf_op jit(solution)/shard_map/psum | solution.py:236
  1138.2 0.7 reduce_sum.186
  1138.9 1.8 convolution_add_fusion.3
  1140.7 0.1 convert_reduce_fusion.4
  1140.8 18.1 %all-reduce.2 = (f32[768]{0:T(1024)S(1)}, f32[768]{0:T(1024)S(1)}, f32[768]{0:T(1024)S(1)}, f32[768]{0:T(1024)S(1)}, f32[768]{0:T(1024)S(1)}, /*index=5*/f32[307...) all-reduce(f32[768]{0:T(1024)S(1)} %copy-done.37, ...), channel_id=1, replica_groups=mesh['dp'=8,'seq'=4] {'seq'}, use_global_device_ids=true, to_apply=%region_16.17 | all-reduce | flops 9216 | bytes 73728 | tf_op jit(solution)/shard_map/psum | solution.py:236
  1158.9 25.9 %all-reduce = (f32[768]{0:T(1024)}, f32[768]{0:T(1024)}, f32[768]{0:T(1024)}, f32[768]{0:T(1024)}, f32[768]{0:T(1024)}, /*index=5*/f32[3072]{0:T(1024)}, f32[768]{0:T(1024)}, f32[768]{0:T(1024)}, f32[768]{0:T(1024)}) all-reduce(f32[768]{0:T(1024)S(1)} %get-tuple-element.134, ...), channel_id=1, replica_groups=mesh['dp'=8,'seq'=4] {'dp'}, use_global_device_ids=true, to_apply=%region_17.18 | all-reduce | flops 9216 | bytes 73728 | tf_op jit(solution)/shard_map/psum | solution.py:235
  1184.7 1.6 convolution_add_fusion.2
  1186.4 1.3 fusion.22
  1187.6 301.0 %all-reduce.7.cloned.1.call-done = (f32[768,768]{0,1:T(8,128)}, f32[768,768]{0,1:T(8,128)}, f32[768,768]{0,1:T(8,128)}, f32[768,768]{1,0:T(8,128)}, f32[768,3072]{1,0:T(8,128)}, /*index=5*/f32[3072,768]{1,0:T(8,128)}) async-done(((f32[768,768]{0,1:T(8,128)}, f32[768,768]{0,1:T(8,128)}, f32[768,768]{0,1:T(8,128)}, f32[768,768]{1,0:T(8,128)}, f32[768,3072]{1,0:T(8,128)}, /*index=5*/f32[3072,768]{1,0:T(8,128)}), ...) | async-done | bytes 28311568 | tf_op jit(solution)/shard_map/psum | solution.py:235
  1488.6 3.2 copy.57
  1491.8 1.9 copy.58
  1493.7 3.2 copy.59
  1496.9 1.4 copy.105
  1498.3 9.3 copy.106
  1507.7 3.7 copy.107
  (124 shorter events, 0.6 us)
Async XLA Ops:
  7.2 87.9 %copy-start = (bf16[768,768]{1,0:T(8,128)(2,1)S(1)}, bf16[768,768]{1,0:T(8,128)(2,1)}, u32[]{:S(2)}) copy-start(bf16[768,768]{1,0:T(8,128)(2,1)} %param.25) | copy-start | bytes 3538948
  7.2 71.3 %all-gather.2.cloned.1.call-start = ((), (), s32[]{:S(2)}) async-start(), calls=%async_computation.2 | async-start | bytes 3932160 | tf_op jit(solution)/shard_map/all_gather | solution.py:157
  7.3 5.0 copy-start.6
  7.3 5.0 copy-start.27
  7.3 5.0 copy-start.43
  11.1 1.9 copy-start.41
  11.2 14.5 copy-start.11
  11.2 14.5 copy-start.31
  12.2 144.9 %reduce-scatter.3.cloned.1.call-start = ((), (), s32[]{:S(2)}) async-start(), calls=%async_computation.3 | async-start | bytes 1966080 | tf_op jit(solution)/shard_map/reduce_scatter | solution.py:214
  13.0 73.5 %copy-start.9 = (bf16[2,128,12,64]{1,0,3,2:T(2,128)(2,1)}, bf16[2,128,12,64]{1,0,3,2:T(2,128)(2,1)S(1)}, u32[]{:S(2)}) copy-start(bf16[2,128,12,64]{1,0,3,2:T(2,128)(2,1)S(1)} %reshape.206) | copy-start | bytes 1179652
  86.5 2.3 copy-start.25
  88.8 2.7 copy-start.2
  88.8 2.7 copy-start.20
  91.5 4.5 slice-start.5
  91.5 3.6 copy-start.44
  91.5 4.5 slice-start.6
  94.7 1.3 copy-start.29
  94.7 1.3 copy-start.30
  94.7 1.4 copy-start.42
  95.1 2.8 copy-start.21
  95.1 2.8 slice-start.3
  95.7 11.9 copy-start.4
  95.7 11.9 copy-start.32
  96.0 11.6 copy-start.38
  96.0 1.9 slice-start.4
  96.1 1.9 copy-start.45
  97.9 1.6 copy-start.16
  98.0 1.8 copy-start.12
  98.0 2.7 copy-start.40
  102.4 3.0 copy-start.14
  105.4 2.2 copy-start.23
  112.3 6.3 copy-start.10
  116.9 1.7 copy-start.3
  120.3 2.7 copy-start.26
  120.3 2.7 copy-start.36
  123.0 71.3 %reduce-scatter.5.cloned.1.call-start = ((), (), s32[]{:S(2)}) async-start(), calls=%async_computation.4 | async-start | bytes 1966080 | tf_op jit(solution)/shard_map/reduce_scatter | solution.py:217
  131.2 3.7 copy-start.7
  131.2 1007.0 %all-reduce.9.cloned.1.call-start = ((), (), s32[]{:S(2)}) async-start(), calls=%async_computation.6 | async-start | bytes 56623104 | tf_op jit(solution)/shard_map/psum | solution.py:236
  134.4 2.3 copy-start.22
  134.9 3.8 copy-start.15
  134.9 3.8 copy-start.17
  138.7 5.2 copy-start.5
  138.7 5.2 copy-start.24
  138.7 5.2 copy-start.33
  138.7 5.2 copy-start.39
  197.2 1291.4 %all-reduce.7.cloned.1.call-start = ((), (), s32[]{:S(2)}) async-start(), calls=%async_computation.5 | async-start | bytes 56623104 | tf_op jit(solution)/shard_map/psum | solution.py:235
  1138.2 2.5 copy-start.13
  1138.2 2.6 copy-start.34
  1138.2 2.6 copy-start.35
  1138.2 46.5 %copy-start.8 = (bf16[768,768]{1,0:T(8,128)(2,1)S(1)}, bf16[768,768]{1,0:T(8,128)(2,1)}, u32[]{:S(2)}) copy-start(bf16[768,768]{1,0:T(8,128)(2,1)} %param.22) | copy-start | bytes 3538948
  1138.9 1.9 copy-start.37
  1184.7 1.6 copy-start.28
  1488.6 3.2 copy-start.19
  1493.7 3.2 copy-start.18
  1496.9 10.7 slice-start
  1498.3 9.3 slice-start.1
  1498.3 9.3 slice-start.2
  1507.7 3.8 copy-start.1
Sparse Core Ops, SparseCore 0:
  12.3 66.1 all-gather.1
  123.1 33.9 reduce-scatter.2
  160.0 34.2 reduce-scatter.4
  198.6 939.5 all-reduce.8
  1143.6 344.9 all-reduce.6
